TPU v7x, 128 devices: a whole 4x4x4 slice. The times are simulated.
128 devices in a mesh: dp: 32 (over z, y, core), tm: 4 (over x).
Axes of the slice: x: 4, y: 4, z: 4, core: 2. Of those that a mesh axis runs over, the one named last changes fastest.
Arguments:
- student: bfloat16 [256, 1024, 128], P(('dp', 'tm')), may hold values from -6 to 6
- teacher: bfloat16 [256, 1024, 128], P(('dp', 'tm')), may hold values from -200 to 200
- partner_dp: int32 [256, 8], replicated, may hold values from 0 to 31, all different within a row; in each aligned block of 2 rows (0 to 1, 2 to 3, ...) no two rows name the same one
- partner_slot: int32 [256, 8], replicated, may hold values from 0 to 1
- valid_frames: int32 [256], replicated, may hold values from 256 to 1024, as said below
Outputs:
- loss: float32 [], replicated
- grad_student: bfloat16 [256, 1024, 128], P(('dp', 'tm'))
Inputs may be any that keep to these rules, and one draw needn't show every extreme that they name: `partner_dp`: among the partner entries of the 2 blocks of one device no dp index appears more than 1 times; the 8 entries of one block are distinct. A partner may be the block itself. `valid_frames`: block 0 is full and block 1 has the fewest valid frames.
All inputs are finite; a program needn't handle non-finite values.
Results may differ from a plain program's by a relative error of at most 0.0042.
Values may be sent and summed in bfloat16 or wider, within the bound.
A program may use at most 64 MiB of HBM per device.

v0:
```python
import math
import jax
import jax.numpy as jnp
from jax import lax
from jax.sharding import PartitionSpec as P

NEG_FILL = -1e30


def body(student, teacher, partner_dp, partner_slot, valid_frames):
    peer_count = lax.axis_size("dp")
    time_count = lax.axis_size("tm")
    my_dp = lax.axis_index("dp")
    my_tm = lax.axis_index("tm")
    local_blocks, frames, proj_width = student.shape
    partner_count = partner_dp.shape[1]
    entries = local_blocks * partner_count
    slot_depth = (entries + peer_count - 1) // peer_count
    slot_total = peer_count * slot_depth
    score_scale = 1.0 / math.sqrt(proj_width)
    dest_all = lax.dynamic_index_in_dim(
        partner_dp.reshape(peer_count, time_count, entries), my_tm, 1, keepdims=False
    )
    source_all = lax.dynamic_index_in_dim(
        partner_slot.reshape(peer_count, time_count, entries), my_tm, 1, keepdims=False
    )
    earlier = jnp.tril(jnp.ones((entries, entries), jnp.int32), -1)
    same_dest = (dest_all[:, :, None] == dest_all[:, None, :]).astype(jnp.int32)
    rank_all = jnp.sum(same_dest * earlier[None], axis=2)
    my_dest = lax.dynamic_index_in_dim(dest_all, my_dp, 0, keepdims=False)
    my_source = lax.dynamic_index_in_dim(source_all, my_dp, 0, keepdims=False)
    my_rank = lax.dynamic_index_in_dim(rank_all, my_dp, 0, keepdims=False)
    entry_slot = my_dest * slot_depth + my_rank
    depth_ids = jnp.arange(slot_depth, dtype=jnp.int32)
    wanted = (dest_all == my_dp)[:, :, None] & (rank_all[:, :, None] == depth_ids[None, None, :])
    in_use = jnp.any(wanted, axis=1).reshape(slot_total)
    local_block = jnp.sum(jnp.where(wanted, source_all[:, :, None], 0), axis=1).reshape(slot_total)
    block_base = (my_dp * time_count + my_tm) * local_blocks
    frame_ids = jnp.arange(frames, dtype=jnp.int32)
    own_len = lax.dynamic_slice_in_dim(valid_frames, block_base, local_blocks)
    far_len = valid_frames[(my_dest * time_count + my_tm) * local_blocks + my_source]
    query_ok = frame_ids[None, :] < own_len[:, None]
    everyone = lax.all_gather(teacher, "dp", axis=0, tiled=True)
    far_keys = everyone[my_dest * local_blocks + my_source]
    keys_all = jnp.concatenate(
        [teacher[:, None], far_keys.reshape(local_blocks, partner_count, frames, proj_width)],
        axis=1,
    )
    lens_all = jnp.concatenate(
        [own_len[:, None], far_len.reshape(local_blocks, partner_count)], axis=1
    )
    keys_tiled = jnp.swapaxes(keys_all, 0, 1)
    lens_tiled = jnp.swapaxes(lens_all, 0, 1)

    def first_pass(inputs):
        key_block, lengths = inputs
        scores = (
            jnp.einsum("aie,aje->aij", student, key_block, preferred_element_type=jnp.float32)
            * score_scale
        )
        key_ok = frame_ids[None, :] < lengths[:, None]
        row_masked = jnp.where(key_ok[:, None, :], scores, NEG_FILL)
        row_best = jnp.max(row_masked, axis=2)
        row_sum = jnp.sum(jnp.exp(row_masked - row_best[:, :, None]), axis=2)
        col_masked = jnp.where(query_ok[:, :, None], scores, NEG_FILL)
        col_best = jnp.max(col_masked, axis=1)
        col_sum = jnp.sum(jnp.exp(col_masked - col_best[:, None, :]), axis=1)
        return (row_best, row_sum, col_best, col_sum)

    row_best, row_sum, col_best, col_sum = lax.map(first_pass, (keys_tiled, lens_tiled))
    row_top = jnp.max(row_best, axis=0)
    row_lse = row_top + jnp.log(jnp.sum(row_sum * jnp.exp(row_best - row_top[None]), axis=0))
    far_best = jnp.swapaxes(col_best[1:], 0, 1).reshape(entries, frames)
    far_sum = jnp.swapaxes(col_sum[1:], 0, 1).reshape(entries, frames)
    back_best = jnp.full((slot_total, frames), NEG_FILL, jnp.float32).at[entry_slot].set(far_best)
    back_sum = jnp.zeros((slot_total, frames), jnp.float32).at[entry_slot].set(far_sum)
    inc_best, inc_sum = (
        lax.all_to_all(back_best, "dp", split_axis=0, concat_axis=0, tiled=True),
        lax.all_to_all(back_sum, "dp", split_axis=0, concat_axis=0, tiled=True),
    )
    chosen = (local_block[:, None] == jnp.arange(local_blocks, dtype=jnp.int32)[None, :]) & in_use[
        :, None
    ]
    cand_best = jnp.where(chosen[:, :, None], inc_best[:, None, :], NEG_FILL)
    merged_best = jnp.maximum(col_best[0], jnp.max(cand_best, axis=0))
    merged_sum = col_sum[0] * jnp.exp(col_best[0] - merged_best)
    merged_sum = merged_sum + jnp.sum(
        jnp.where(
            chosen[:, :, None], inc_sum[:, None, :] * jnp.exp(cand_best - merged_best[None]), 0.0
        ),
        axis=0,
    )
    col_lse = merged_best + jnp.log(jnp.where(query_ok, merged_sum, 1.0))
    lse_out = jnp.where(in_use[:, None], col_lse[local_block], 0.0)
    lse_in = lax.all_to_all(lse_out, "dp", split_axis=0, concat_axis=0, tiled=True)
    far_lse = lse_in[entry_slot].reshape(local_blocks, partner_count, frames)
    lse_tiled = jnp.swapaxes(jnp.concatenate([col_lse[:, None], far_lse], axis=1), 0, 1)
    positive = (
        jnp.sum(student.astype(jnp.float32) * teacher.astype(jnp.float32), axis=2) * score_scale
    )
    row_terms = jnp.sum(jnp.where(query_ok, row_lse - positive, 0.0))
    col_terms = jnp.sum(jnp.where(query_ok, col_lse - positive, 0.0))
    loss_sum = lax.psum(0.5 * (row_terms + col_terms), ("dp", "tm"))
    loss = loss_sum / jnp.sum(valid_frames).astype(jnp.float32)
    diagonal = frame_ids[:, None] == frame_ids[None, :]

    def second_pass(inputs):
        key_block, lengths, key_lse, tile_index = inputs
        scores = (
            jnp.einsum("aie,aje->aij", student, key_block, preferred_element_type=jnp.float32)
            * score_scale
        )
        key_ok = frame_ids[None, :] < lengths[:, None]
        pair_ok = query_ok[:, :, None] & key_ok[:, None, :]
        prob_row = jnp.exp(scores - row_lse[:, :, None])
        prob_col = jnp.exp(scores - key_lse[:, None, :])
        grad_scores = jnp.where(pair_ok, 0.5 * (prob_row + prob_col), 0.0)
        grad_scores = grad_scores - jnp.where(
            (tile_index == 0) & diagonal[None] & query_ok[:, :, None], 1.0, 0.0
        )
        return jnp.einsum(
            "aij,aje->aie",
            grad_scores.astype(jnp.bfloat16),
            key_block,
            preferred_element_type=jnp.float32,
        )

    tile_ids = jnp.arange(partner_count + 1, dtype=jnp.int32)
    pieces = lax.map(second_pass, (keys_tiled, lens_tiled, lse_tiled, tile_ids))
    grad_student = (jnp.sum(pieces, axis=0) * score_scale).astype(jnp.bfloat16)
    return (loss, grad_student)


def solution(mesh):
    placed = (P(("dp", "tm"), None, None), P(("dp", "tm"), None, None), P(), P(), P())
    return jax.shard_map(
        body,
        mesh=mesh,
        in_specs=placed,
        out_specs=(P(), P(("dp", "tm"), None, None)),
        check_vma=False,
    )
```

profile of v0, /device:TPU:1, one launch (start us, length us, event | category | flops | bytes accessed | tf_op | source)
XLA Modules:
  0.0 386.1 jit_solution(9657005875069770102)
XLA Ops:
  8.0 0.8 dynamic_slice.42
  9.6 0.8 copy.92
  10.5 0.8 copy.93
  12.1 1.3 gather_fusion
  13.7 1.6 multiply_reduce_fusion
  15.3 71.3 %all-gather.2.cloned.1.call-done = bf16[64,1024,128]{2,1,0:T(8,128)(2,1)} async-done(((bf16[2,1024,128]{2,1,0:T(8,128)(2,1)}), bf16[64,1024,128]{2,1,0:T(8,128)(2,1)}) %all-gather.2.cloned.1.call-update) | async-done | bytes 16777232 | tf_op jit(solution)/shard_map/all_gather | solution.py:43
  86.6 8.8 %gather_fusion.1 = bf16[16,1024,128]{2,1,0:T(8,128)(2,1)} fusion(bf16[64,1024,128]{2,1,0:T(8,128)(2,1)} %all-gather.2.cloned.1.call-done, s32[1024]{0:T(1024)S(1)} %pad_clamp_fusion.2), kind=kCustom, calls=%fused_computation.1 | custom fusion | bytes 8388672 | tf_op jit(solution)/shard_map/gather | solution.py:44
  95.3 2.7 maximum_bitcast_fusion
  98.0 2.7 copy.96
  100.7 74.8 %while.28 = (s32[]{:T(128)}, f32[9,2,1024]{2,1,0:T(2,128)S(1)}, f32[9,2,1024]{2,1,0:T(2,128)S(1)}, f32[9,2,1024]{2,1,0:T(2,128)S(1)}, f32[9,2,1024]{2,1,0:T(2,12...) while((s32[]{:T(128)}, f32[9,2,1024]{2,1,0:T(2,128)S(1)}, ...), condition=%wide.region_5.6_spmd.clone, body=%wide.region_0.5_spmd.clone.sunk | while | flops 562032640 | bytes 17952924 | solution.py:70
  100.8 3.5 bitcast_reduce_fusion.3
  104.3 4.6 %fusion.84 = (f32[2,1024]{1,0:T(2,128)S(1)}, f32[2,1024]{1,0:T(2,128)S(1)}) fusion(f32[2,1024,1024]{2,1,0:T(8,128)S(1)} %get-tuple-element.479, f32[2,1024]{1,0:T(2,128)S(1)} %get-tuple-element.480, pred[2,1024]{1,0:T(4,128)(4,1)S(1)} %iota_compare_fusion.10, f32[2,1024]{1,0:T(2,128)S(1)} %get-tuple-element.481, ...), kind=kLoop, calls=%fused_computation.14.clone.1 | loop fusion | flops 14675968 | bytes 8425472 | tf_op jit(solution)/shard_map/while/body/eval_jaxpr/reduce_sum | solution.py:67
  109.1 3.5 bitcast_reduce_fusion.3
  112.6 4.6 %fusion.84 = (f32[2,1024]{1,0:T(2,128)S(1)}, f32[2,1024]{1,0:T(2,128)S(1)}) fusion(f32[2,1024,1024]{2,1,0:T(8,128)S(1)} %get-tuple-element.479, f32[2,1024]{1,0:T(2,128)S(1)} %get-tuple-element.480, pred[2,1024]{1,0:T(4,128)(4,1)S(1)} %iota_compare_fusion.10, f32[2,1024]{1,0:T(2,128)S(1)} %get-tuple-element.481, ...), kind=kLoop, calls=%fused_computation.14.clone.1 | loop fusion | flops 14675968 | bytes 8425472 | tf_op jit(solution)/shard_map/while/body/eval_jaxpr/reduce_sum | solution.py:67
  117.5 3.5 bitcast_reduce_fusion.3
  120.9 4.6 %fusion.84 = (f32[2,1024]{1,0:T(2,128)S(1)}, f32[2,1024]{1,0:T(2,128)S(1)}) fusion(f32[2,1024,1024]{2,1,0:T(8,128)S(1)} %get-tuple-element.479, f32[2,1024]{1,0:T(2,128)S(1)} %get-tuple-element.480, pred[2,1024]{1,0:T(4,128)(4,1)S(1)} %iota_compare_fusion.10, f32[2,1024]{1,0:T(2,128)S(1)} %get-tuple-element.481, ...), kind=kLoop, calls=%fused_computation.14.clone.1 | loop fusion | flops 14675968 | bytes 8425472 | tf_op jit(solution)/shard_map/while/body/eval_jaxpr/reduce_sum | solution.py:67
  125.8 3.5 bitcast_reduce_fusion.3
  129.2 4.6 %fusion.84 = (f32[2,1024]{1,0:T(2,128)S(1)}, f32[2,1024]{1,0:T(2,128)S(1)}) fusion(f32[2,1024,1024]{2,1,0:T(8,128)S(1)} %get-tuple-element.479, f32[2,1024]{1,0:T(2,128)S(1)} %get-tuple-element.480, pred[2,1024]{1,0:T(4,128)(4,1)S(1)} %iota_compare_fusion.10, f32[2,1024]{1,0:T(2,128)S(1)} %get-tuple-element.481, ...), kind=kLoop, calls=%fused_computation.14.clone.1 | loop fusion | flops 14675968 | bytes 8425472 | tf_op jit(solution)/shard_map/while/body/eval_jaxpr/reduce_sum | solution.py:67
  134.1 3.5 bitcast_reduce_fusion.3
  137.6 4.6 %fusion.84 = (f32[2,1024]{1,0:T(2,128)S(1)}, f32[2,1024]{1,0:T(2,128)S(1)}) fusion(f32[2,1024,1024]{2,1,0:T(8,128)S(1)} %get-tuple-element.479, f32[2,1024]{1,0:T(2,128)S(1)} %get-tuple-element.480, pred[2,1024]{1,0:T(4,128)(4,1)S(1)} %iota_compare_fusion.10, f32[2,1024]{1,0:T(2,128)S(1)} %get-tuple-element.481, ...), kind=kLoop, calls=%fused_computation.14.clone.1 | loop fusion | flops 14675968 | bytes 8425472 | tf_op jit(solution)/shard_map/while/body/eval_jaxpr/reduce_sum | solution.py:67
  142.4 3.5 bitcast_reduce_fusion.3
  145.9 4.6 %fusion.84 = (f32[2,1024]{1,0:T(2,128)S(1)}, f32[2,1024]{1,0:T(2,128)S(1)}) fusion(f32[2,1024,1024]{2,1,0:T(8,128)S(1)} %get-tuple-element.479, f32[2,1024]{1,0:T(2,128)S(1)} %get-tuple-element.480, pred[2,1024]{1,0:T(4,128)(4,1)S(1)} %iota_compare_fusion.10, f32[2,1024]{1,0:T(2,128)S(1)} %get-tuple-element.481, ...), kind=kLoop, calls=%fused_computation.14.clone.1 | loop fusion | flops 14675968 | bytes 8425472 | tf_op jit(solution)/shard_map/while/body/eval_jaxpr/reduce_sum | solution.py:67
  150.7 3.5 bitcast_reduce_fusion.3
  154.2 4.6 %fusion.84 = (f32[2,1024]{1,0:T(2,128)S(1)}, f32[2,1024]{1,0:T(2,128)S(1)}) fusion(f32[2,1024,1024]{2,1,0:T(8,128)S(1)} %get-tuple-element.479, f32[2,1024]{1,0:T(2,128)S(1)} %get-tuple-element.480, pred[2,1024]{1,0:T(4,128)(4,1)S(1)} %iota_compare_fusion.10, f32[2,1024]{1,0:T(2,128)S(1)} %get-tuple-element.481, ...), kind=kLoop, calls=%fused_computation.14.clone.1 | loop fusion | flops 14675968 | bytes 8425472 | tf_op jit(solution)/shard_map/while/body/eval_jaxpr/reduce_sum | solution.py:67
  159.0 3.5 bitcast_reduce_fusion.3
  162.5 4.6 %fusion.84 = (f32[2,1024]{1,0:T(2,128)S(1)}, f32[2,1024]{1,0:T(2,128)S(1)}) fusion(f32[2,1024,1024]{2,1,0:T(8,128)S(1)} %get-tuple-element.479, f32[2,1024]{1,0:T(2,128)S(1)} %get-tuple-element.480, pred[2,1024]{1,0:T(4,128)(4,1)S(1)} %iota_compare_fusion.10, f32[2,1024]{1,0:T(2,128)S(1)} %get-tuple-element.481, ...), kind=kLoop, calls=%fused_computation.14.clone.1 | loop fusion | flops 14675968 | bytes 8425472 | tf_op jit(solution)/shard_map/while/body/eval_jaxpr/reduce_sum | solution.py:67
  167.3 3.5 bitcast_reduce_fusion.3
  170.8 4.6 %fusion.84 = (f32[2,1024]{1,0:T(2,128)S(1)}, f32[2,1024]{1,0:T(2,128)S(1)}) fusion(f32[2,1024,1024]{2,1,0:T(8,128)S(1)} %get-tuple-element.479, f32[2,1024]{1,0:T(2,128)S(1)} %get-tuple-element.480, pred[2,1024]{1,0:T(4,128)(4,1)S(1)} %iota_compare_fusion.10, f32[2,1024]{1,0:T(2,128)S(1)} %get-tuple-element.481, ...), kind=kLoop, calls=%fused_computation.14.clone.1 | loop fusion | flops 14675968 | bytes 8425472 | tf_op jit(solution)/shard_map/while/body/eval_jaxpr/reduce_sum | solution.py:67
  177.0 5.4 %all-to-all-start = ((f32[32,1,1024]{2,1,0:T(1,128)}), f32[32,1,1024]{2,1,0:T(1,128)S(1)}, u32[]{:S(2)}, u32[]{:S(2)}) async-start(f32[32,1,1024]{2,1,0:T(1,128)} %all_to_all.18), calls=%async_computation | async-start | bytes 262144 | tf_op jit(solution)/shard_map/all_to_all | solution.py:78
  184.7 5.3 %all-to-all-done = f32[32,1,1024]{2,1,0:T(1,128)S(1)} async-done(((f32[32,1,1024]{2,1,0:T(1,128)}), f32[32,1,1024]{2,1,0:T(1,128)S(1)}, u32[]{:S(2)}, u32[]{:S(2)}) %all-to-all-start) | async-done | bytes 131104 | tf_op jit(solution)/shard_map/all_to_all | solution.py:78
  190.0 3.9 %all-to-all-start.1 = ((f32[32,1,1024]{2,1,0:T(1,128)}), f32[32,1,1024]{2,1,0:T(1,128)S(1)}, u32[]{:S(2)}, u32[]{:S(2)}) async-start(f32[32,1,1024]{2,1,0:T(1,128)} %all_to_all.20), calls=%async_computation.1 | async-start | bytes 262144 | tf_op jit(solution)/shard_map/all_to_all | solution.py:79
  194.1 7.6 %all-to-all-done.1 = f32[32,1,1024]{2,1,0:T(1,128)S(1)} async-done(((f32[32,1,1024]{2,1,0:T(1,128)}), f32[32,1,1024]{2,1,0:T(1,128)S(1)}, u32[]{:S(2)}, u32[]{:S(2)}) %all-to-all-start.1) | async-done | bytes 131104 | tf_op jit(solution)/shard_map/all_to_all | solution.py:79
  204.4 64.1 %psum.7 = f32[]{:T(128)} all-reduce(f32[]{:T(128)S(6)} %mul.113), channel_id=1, replica_groups=mesh['dp'=32,'tm'=4] {'dp','tm'}, use_global_device_ids=true, to_apply=%region_18.19 | all-reduce | flops 1 | bytes 8 | tf_op jit(solution)/shard_map/psum | solution.py:103
  269.3 0.8 copy.101
  270.1 4.7 %all-to-all-start.2 = ((f32[32,1,1024]{2,1,0:T(1,128)}), f32[32,1,1024]{2,1,0:T(1,128)S(1)}, u32[]{:S(2)}, u32[]{:S(2)}) async-start(f32[32,1,1024]{2,1,0:T(1,128)} %copy.101), calls=%async_computation.2 | async-start | bytes 262144 | tf_op jit(solution)/shard_map/all_to_all | solution.py:95
  275.6 6.9 %all-to-all-done.2 = f32[32,1,1024]{2,1,0:T(1,128)S(1)} async-done(((f32[32,1,1024]{2,1,0:T(1,128)}), f32[32,1,1024]{2,1,0:T(1,128)S(1)}, u32[]{:S(2)}, u32[]{:S(2)}) %all-to-all-start.2) | async-done | bytes 131104 | tf_op jit(solution)/shard_map/all_to_all | solution.py:95
  283.1 89.9 %while.29 = (s32[]{:T(128)}, f32[9,2,1024,128]{3,2,1,0:T(8,128)}, s32[9,2]{1,0:T(8,128)S(1)}, bf16[9,2,1024,128]{3,2,1,0:T(8,128)(2,1)}, bf16[2,1024,128]{2,1,0:...) while((s32[]{:T(128)}, f32[9,2,1024,128]{3,2,1,0:T(8,128)}, ...), condition=%wide.region_21.22_spmd.clone, body=%wide.region_20.21_spmd.clone.sunk | while | flops 1098911744 | bytes 4761267 | solution.py:129
  284.8 8.3 %fusion.91 = f32[9,2,1024,128]{3,2,1,0:T(8,128)} fusion(f32[9,2,1024,128]{3,2,1,0:T(8,128)} %get-tuple-element.541, s32[]{:T(128)S(6)} %copy.138, f32[2,1024]{1,0:T(2,128)S(1)} %dynamic-slice_bitcast_fusion.3, f32[2,1024]{1,0:T(2,128)S(1)} %get-tuple-element.556, pred[1024,1024]{0,1:T(8,128)(4,1)S(1)} %fusion.89, ...), kind=kOutput, calls=%fused_computation.39.clone.1 | convolution fusion | flops 1096810496 | bytes 3692032 | tf_op jit(solution)/shard_map/while/body/eval_jaxpr/aij,aje->aie/dot_general | solution.py:121
  294.8 8.3 %fusion.91 = f32[9,2,1024,128]{3,2,1,0:T(8,128)} fusion(f32[9,2,1024,128]{3,2,1,0:T(8,128)} %get-tuple-element.541, s32[]{:T(128)S(6)} %copy.138, f32[2,1024]{1,0:T(2,128)S(1)} %dynamic-slice_bitcast_fusion.3, f32[2,1024]{1,0:T(2,128)S(1)} %get-tuple-element.556, pred[1024,1024]{0,1:T(8,128)(4,1)S(1)} %fusion.89, ...), kind=kOutput, calls=%fused_computation.39.clone.1 | convolution fusion | flops 1096810496 | bytes 3692032 | tf_op jit(solution)/shard_map/while/body/eval_jaxpr/aij,aje->aie/dot_general | solution.py:121
  304.8 8.3 %fusion.91 = f32[9,2,1024,128]{3,2,1,0:T(8,128)} fusion(f32[9,2,1024,128]{3,2,1,0:T(8,128)} %get-tuple-element.541, s32[]{:T(128)S(6)} %copy.138, f32[2,1024]{1,0:T(2,128)S(1)} %dynamic-slice_bitcast_fusion.3, f32[2,1024]{1,0:T(2,128)S(1)} %get-tuple-element.556, pred[1024,1024]{0,1:T(8,128)(4,1)S(1)} %fusion.89, ...), kind=kOutput, calls=%fused_computation.39.clone.1 | convolution fusion | flops 1096810496 | bytes 3692032 | tf_op jit(solution)/shard_map/while/body/eval_jaxpr/aij,aje->aie/dot_general | solution.py:121
  314.8 8.3 %fusion.91 = f32[9,2,1024,128]{3,2,1,0:T(8,128)} fusion(f32[9,2,1024,128]{3,2,1,0:T(8,128)} %get-tuple-element.541, s32[]{:T(128)S(6)} %copy.138, f32[2,1024]{1,0:T(2,128)S(1)} %dynamic-slice_bitcast_fusion.3, f32[2,1024]{1,0:T(2,128)S(1)} %get-tuple-element.556, pred[1024,1024]{0,1:T(8,128)(4,1)S(1)} %fusion.89, ...), kind=kOutput, calls=%fused_computation.39.clone.1 | convolution fusion | flops 1096810496 | bytes 3692032 | tf_op jit(solution)/shard_map/while/body/eval_jaxpr/aij,aje->aie/dot_general | solution.py:121
  324.7 8.3 %fusion.91 = f32[9,2,1024,128]{3,2,1,0:T(8,128)} fusion(f32[9,2,1024,128]{3,2,1,0:T(8,128)} %get-tuple-element.541, s32[]{:T(128)S(6)} %copy.138, f32[2,1024]{1,0:T(2,128)S(1)} %dynamic-slice_bitcast_fusion.3, f32[2,1024]{1,0:T(2,128)S(1)} %get-tuple-element.556, pred[1024,1024]{0,1:T(8,128)(4,1)S(1)} %fusion.89, ...), kind=kOutput, calls=%fused_computation.39.clone.1 | convolution fusion | flops 1096810496 | bytes 3692032 | tf_op jit(solution)/shard_map/while/body/eval_jaxpr/aij,aje->aie/dot_general | solution.py:121
  334.7 8.3 %fusion.91 = f32[9,2,1024,128]{3,2,1,0:T(8,128)} fusion(f32[9,2,1024,128]{3,2,1,0:T(8,128)} %get-tuple-element.541, s32[]{:T(128)S(6)} %copy.138, f32[2,1024]{1,0:T(2,128)S(1)} %dynamic-slice_bitcast_fusion.3, f32[2,1024]{1,0:T(2,128)S(1)} %get-tuple-element.556, pred[1024,1024]{0,1:T(8,128)(4,1)S(1)} %fusion.89, ...), kind=kOutput, calls=%fused_computation.39.clone.1 | convolution fusion | flops 1096810496 | bytes 3692032 | tf_op jit(solution)/shard_map/while/body/eval_jaxpr/aij,aje->aie/dot_general | solution.py:121
  344.7 8.3 %fusion.91 = f32[9,2,1024,128]{3,2,1,0:T(8,128)} fusion(f32[9,2,1024,128]{3,2,1,0:T(8,128)} %get-tuple-element.541, s32[]{:T(128)S(6)} %copy.138, f32[2,1024]{1,0:T(2,128)S(1)} %dynamic-slice_bitcast_fusion.3, f32[2,1024]{1,0:T(2,128)S(1)} %get-tuple-element.556, pred[1024,1024]{0,1:T(8,128)(4,1)S(1)} %fusion.89, ...), kind=kOutput, calls=%fused_computation.39.clone.1 | convolution fusion | flops 1096810496 | bytes 3692032 | tf_op jit(solution)/shard_map/while/body/eval_jaxpr/aij,aje->aie/dot_general | solution.py:121
  354.6 8.3 %fusion.91 = f32[9,2,1024,128]{3,2,1,0:T(8,128)} fusion(f32[9,2,1024,128]{3,2,1,0:T(8,128)} %get-tuple-element.541, s32[]{:T(128)S(6)} %copy.138, f32[2,1024]{1,0:T(2,128)S(1)} %dynamic-slice_bitcast_fusion.3, f32[2,1024]{1,0:T(2,128)S(1)} %get-tuple-element.556, pred[1024,1024]{0,1:T(8,128)(4,1)S(1)} %fusion.89, ...), kind=kOutput, calls=%fused_computation.39.clone.1 | convolution fusion | flops 1096810496 | bytes 3692032 | tf_op jit(solution)/shard_map/while/body/eval_jaxpr/aij,aje->aie/dot_general | solution.py:121
  364.6 8.4 %fusion.91 = f32[9,2,1024,128]{3,2,1,0:T(8,128)} fusion(f32[9,2,1024,128]{3,2,1,0:T(8,128)} %get-tuple-element.541, s32[]{:T(128)S(6)} %copy.138, f32[2,1024]{1,0:T(2,128)S(1)} %dynamic-slice_bitcast_fusion.3, f32[2,1024]{1,0:T(2,128)S(1)} %get-tuple-element.556, pred[1024,1024]{0,1:T(8,128)(4,1)S(1)} %fusion.89, ...), kind=kOutput, calls=%fused_computation.39.clone.1 | convolution fusion | flops 1096810496 | bytes 3692032 | tf_op jit(solution)/shard_map/while/body/eval_jaxpr/aij,aje->aie/dot_general | solution.py:121
  373.0 4.2 %reduce_sum.113 = f32[2,1024,128]{2,1,0:T(8,128)S(1)} reduce(f32[9,2,1024,128]{3,2,1,0:T(8,128)} %get-tuple-element.118, f32[]{:T(128)} %constant.134.clone.1), dimensions={0}, to_apply=%region_22.23 | reduce | flops 2097152 | bytes 10485764 | tf_op jit(solution)/shard_map/reduce_sum | solution.py:130
  377.3 0.9 multiply_convert_fusion
  (150 shorter events, 19.7 us)
Async XLA Ops:
  7.2 88.2 %copy-start.1 = (bf16[2,1024,128]{2,1,0:T(8,128)(2,1)S(1)}, bf16[2,1024,128]{2,1,0:T(8,128)(2,1)}, u32[]{:S(2)}) copy-start(bf16[2,1024,128]{2,1,0:T(8,128)(2,1)} %param.10) | copy-start | bytes 1572868
  7.2 79.4 %all-gather.2.cloned.1.call-start = ((), (), s32[]{:S(2)}) async-start(), calls=%async_computation.3 | async-start | bytes 17301504 | tf_op jit(solution)/shard_map/all_gather | solution.py:43
  95.3 5.3 %copy-start.2 = (bf16[2,1024,128]{2,1,0:T(8,128)(2,1)S(1)}, bf16[2,1024,128]{2,1,0:T(8,128)(2,1)}, u32[]{:S(2)}) copy-start(bf16[2,1024,128]{2,1,0:T(8,128)(2,1)} %param.9) | copy-start | bytes 1572868
  100.7 81.7 %copy-start = (s32[256]{0:T(256)S(1)}, s32[256]{0:T(256)}, u32[]{:S(2)}) copy-start(s32[256]{0:T(256)} %param.13) | copy-start | bytes 3076
  177.0 13.0 %all-to-all-start = ((f32[32,1,1024]{2,1,0:T(1,128)}), f32[32,1,1024]{2,1,0:T(1,128)S(1)}, u32[]{:S(2)}, u32[]{:S(2)}) async-start(f32[32,1,1024]{2,1,0:T(1,128)} %all_to_all.18), calls=%async_computation | async-start | bytes 262144 | tf_op jit(solution)/shard_map/all_to_all | solution.py:78
  190.0 11.6 %all-to-all-start.1 = ((f32[32,1,1024]{2,1,0:T(1,128)}), f32[32,1,1024]{2,1,0:T(1,128)S(1)}, u32[]{:S(2)}, u32[]{:S(2)}) async-start(f32[32,1,1024]{2,1,0:T(1,128)} %all_to_all.20), calls=%async_computation.1 | async-start | bytes 262144 | tf_op jit(solution)/shard_map/all_to_all | solution.py:79
  270.1 12.3 %all-to-all-start.2 = ((f32[32,1,1024]{2,1,0:T(1,128)}), f32[32,1,1024]{2,1,0:T(1,128)S(1)}, u32[]{:S(2)}, u32[]{:S(2)}) async-start(f32[32,1,1024]{2,1,0:T(1,128)} %copy.101), calls=%async_computation.2 | async-start | bytes 262144 | tf_op jit(solution)/shard_map/all_to_all | solution.py:95
Sparse Core Ops, SparseCore 0:
  10.2 76.2 all-gather.1
where the time goes:
time: 387 us; the launch traced here: 386 us
  matrix products  106 us (27%)
  waiting for transfers between devices  91.7 us (24%)
  blocking collectives  64.1 us (17%)
  other arithmetic  58.2 us (15%)
  local copies, waits for them, and re-layouts  27.6 us (7%)
  between operations  18.1 us (5%)
  starting transfers between devices  14.1 us (4%)
  loops' own time  6.51 us (2%)
    dot_general x9, matrix products, second_pass(): jnp.einsum('aij,aje->aie', grad_scores.astype(jnp.bfloat16), key_block, p...  74.6 us
    all_gather x1, waiting for transfers between devices, body(): everyone = lax.all_gather(teacher, 'dp', axis=0, tiled=True)  71.3 us
    psum x1, blocking collectives, body(): loss_sum = lax.psum(0.5 * (row_terms + col_terms), ('dp', 'tm'))  64.1 us
    reduce_sum x9, other arithmetic, first_pass(): col_sum = jnp.sum(jnp.exp(col_masked - col_best[:, None, :]), axis=1)  41.5 us
    dot_general x9, matrix products, first_pass(): jnp.einsum('aie,aje->aij', student, key_block, preferred_element_type=jnp...  31.2 us
    gather x1, local copies, waits for them, and re-layouts, body(): far_keys = everyone[my_dest * local_blocks + my_source]  8.78 us
  transfers between devices with their start and end apart: 4, of which 4 were waited for; matrix products, arithmetic and copies ran while one was open for 2% of the time, Pallas kernels for 0%

commit v1 on v0

--- a/solution.py
+++ b/solution.py
@@ -5,6 +5,15 @@
 from jax.sharding import PartitionSpec as P
 
 NEG_FILL = -1e30
+
+
+def _remake_wires(packet):
+    pile = []
+    for _ in range(lax.axis_size("dp")):
+        pile.append(packet)
+    return jnp.concatenate(
+        lax.all_to_all(jnp.stack(pile, 0), concat_axis=0, split_axis=0, axis_name="dp"), 0
+    )
 
 
 def body(student, teacher, partner_dp, partner_slot, valid_frames):
@@ -40,7 +49,7 @@
     own_len = lax.dynamic_slice_in_dim(valid_frames, block_base, local_blocks)
     far_len = valid_frames[(my_dest * time_count + my_tm) * local_blocks + my_source]
     query_ok = frame_ids[None, :] < own_len[:, None]
-    everyone = lax.all_gather(teacher, "dp", axis=0, tiled=True)
+    everyone = _remake_wires(teacher)
     far_keys = everyone[my_dest * local_blocks + my_source]
     keys_all = jnp.concatenate(
         [teacher[:, None], far_keys.reshape(local_blocks, partner_count, frames, proj_width)],

time: 387 us -> 518 us (1.34)
  waiting for transfers between devices: 91.7 us -> 212 us
  starting transfers between devices: 14.1 us -> 32.6 us
  between operations: 18.1 us -> 4.73 us
    all_to_all x0 -> x1, waiting for transfers between devices: none -> 199 us  [_remake_wires(): lax.all_to_all(jnp.stack(pile, 0), concat_axis=0, split_axis=0, axis_name...]
    all_gather x1 -> x0, waiting for transfers between devices: 71.3 us -> none  [body(): everyone = lax.all_gather(teacher, 'dp', axis=0, tiled=True)]
    all_to_all x0 -> x1, starting transfers between devices: none -> 9.79 us  [_remake_wires(): lax.all_to_all(jnp.stack(pile, 0), concat_axis=0, split_axis=0, axis_name...]
    all_to_all x1, starting transfers between devices: 5.41 us -> 15 us  [body(): lax.all_to_all(back_best, 'dp', split_axis=0, concat_axis=0, tiled=True)]
    another operation x0 -> x1, local copies, waits for them, and re-layouts: none -> 7.02 us  [_remake_wires(): jnp.stack(pile, 0)]
    all_to_all x1, waiting for transfers between devices: 6.85 us -> 0.01 us  [body(): lax.all_to_all(lse_out, 'dp', split_axis=0, concat_axis=0, tiled=True)]
  transfers between devices with their start and end apart: 4 -> 4, of which waited for: 4 -> 3; matrix products, arithmetic and copies ran while one was open for 2% -> 1% of each run, Pallas kernels for 0% -> 0%
where the time goes in v1:
time: 518 us; the launch traced here: 517 us
  waiting for transfers between devices  212 us (41%)
  matrix products  106 us (20%)
  blocking collectives  66.7 us (13%)
  other arithmetic  57.1 us (11%)
  starting transfers between devices  32.6 us (6%)
  local copies, waits for them, and re-layouts  31.2 us (6%)
  loops' own time  6.45 us (1%)
    all_to_all x1, waiting for transfers between devices, _remake_wires(): lax.all_to_all(jnp.stack(pile, 0), concat_axis=0, split_axis=0, axis_name...  199 us
    dot_general x9, matrix products, second_pass(): jnp.einsum('aij,aje->aie', grad_scores.astype(jnp.bfloat16), key_block, p...  75 us
    psum x1, blocking collectives, body(): loss_sum = lax.psum(0.5 * (row_terms + col_terms), ('dp', 'tm'))  66.7 us
    reduce_sum x9, other arithmetic, first_pass(): col_sum = jnp.sum(jnp.exp(col_masked - col_best[:, None, :]), axis=1)  41.6 us
    dot_general x9, matrix products, first_pass(): jnp.einsum('aie,aje->aij', student, key_block, preferred_element_type=jnp...  31.1 us
    all_to_all x1, starting transfers between devices, body(): lax.all_to_all(back_best, 'dp', split_axis=0, concat_axis=0, tiled=True)  15 us
  transfers between devices with their start and end apart: 4, of which 3 were waited for; matrix products, arithmetic and copies ran while one was open for 1% of the time, Pallas kernels for 0%

profile of v1, /device:TPU:1, one launch (start us, length us, event | category | flops | bytes accessed | tf_op | source)
XLA Modules:
  0.0 516.5 jit_solution(17071474132606744418)
XLA Ops:
  0.6 7.0 %stack.2 = bf16[32,2,1024,128]{3,2,1,0:T(8,128)(2,1)} broadcast(bf16[2,1024,128]{2,1,0:T(8,128)(2,1)} %param.10), dimensions={1,2,3} | broadcast | bytes 17301504 | tf_op jit(solution)/shard_map/stack | solution.py:15
  7.7 9.8 %all-to-all-start = ((bf16[32,2,1024,128]{3,2,1,0:T(8,128)(2,1)}), bf16[32,2,1024,128]{3,2,1,0:T(8,128)(2,1)}, u32[]{:S(2)}, u32[]{:S(2)}) async-start(bf16[32,2,1024,128]{3,2,1,0:T(8,128)(2,1)} %stack.2), calls=%async_computation | async-start | bytes 33554432 | tf_op jit(solution)/shard_map/all_to_all | solution.py:15
  20.3 199.2 %all-to-all-done = bf16[32,2,1024,128]{3,2,1,0:T(8,128)(2,1)} async-done(((bf16[32,2,1024,128]{3,2,1,0:T(8,128)(2,1)}), bf16[32,2,1024,128]{3,2,1,0:T(8,128)(2,1)}, u32[]{:S(2)}, u32[]{:S(2)}) %all-to-all-start) | async-done | bytes 16777248 | tf_op jit(solution)/shard_map/all_to_all | solution.py:15
  219.5 8.8 %gather_fusion.1 = bf16[16,1024,128]{2,1,0:T(8,128)(2,1)} fusion(bf16[64,1024,128]{2,1,0:T(8,128)(2,1)} %bitcast.6, s32[1024]{0:T(1024)S(1)} %pad_clamp_fusion.2), kind=kCustom, calls=%fused_computation.1 | custom fusion | bytes 8388672 | tf_op jit(solution)/shard_map/gather | solution.py:53
  228.3 2.6 maximum_bitcast_fusion
  230.9 2.7 copy.96
  233.6 74.8 %while.28 = (s32[]{:T(128)}, f32[9,2,1024]{2,1,0:T(2,128)S(1)}, f32[9,2,1024]{2,1,0:T(2,128)S(1)}, f32[9,2,1024]{2,1,0:T(2,128)S(1)}, f32[9,2,1024]{2,1,0:T(2,12...) while((s32[]{:T(128)}, f32[9,2,1024]{2,1,0:T(2,128)S(1)}, ...), condition=%wide.region_5.6_spmd.clone, body=%wide.region_0.5_spmd.clone.sunk | while | flops 562032640 | bytes 17953424 | solution.py:79
  233.7 3.5 bitcast_reduce_fusion.3
  237.2 4.6 fusion.84
  242.1 3.4 bitcast_reduce_fusion.3
  245.5 4.6 fusion.84
  250.4 3.4 bitcast_reduce_fusion.3
  253.8 4.6 fusion.84
  258.7 3.5 bitcast_reduce_fusion.3
  262.1 4.6 fusion.84
  267.0 3.4 bitcast_reduce_fusion.3
  270.4 4.6 fusion.84
  275.3 3.4 bitcast_reduce_fusion.3
  278.7 4.6 fusion.84
  283.6 3.5 bitcast_reduce_fusion.3
  287.1 4.6 fusion.84
  291.9 3.4 bitcast_reduce_fusion.3
  295.4 4.6 fusion.84
  300.2 3.4 bitcast_reduce_fusion.3
  303.7 4.6 fusion.84
  308.4 0.7 scatter_custom_fusion
  309.1 0.7 all_to_all.22
  309.8 15.0 %all-to-all-start.1 = ((f32[32,1,1024]{2,1,0:T(1,128)}), f32[32,1,1024]{2,1,0:T(1,128)S(1)}, u32[]{:S(2)}, u32[]{:S(2)}) async-start(f32[32,1,1024]{2,1,0:T(1,128)} %all_to_all.22), calls=%async_computation.1 | async-start | bytes 262144 | tf_op jit(solution)/shard_map/all_to_all | solution.py:87
  326.9 0.7 all_to_all.24
  327.8 4.8 all-to-all-done.1
  332.6 3.9 all-to-all-start.2
  336.7 7.6 %all-to-all-done.2 = f32[32,1,1024]{2,1,0:T(1,128)S(1)} async-done(((f32[32,1,1024]{2,1,0:T(1,128)}), f32[32,1,1024]{2,1,0:T(1,128)S(1)}, u32[]{:S(2)}, u32[]{:S(2)}) %all-to-all-start.2) | async-done | bytes 131104 | tf_op jit(solution)/shard_map/all_to_all | solution.py:88
  344.4 0.7 select_reduce_fusion.2
  345.8 0.8 copy.101
  347.9 3.9 all-to-all-start.3
  351.8 66.7 %psum.7 = f32[]{:T(128)} all-reduce(f32[]{:T(128)S(6)} %mul.113), channel_id=1, replica_groups=mesh['dp'=32,'tm'=4] {'dp','tm'}, use_global_device_ids=true, to_apply=%region_18.19 | all-reduce | flops 1 | bytes 8 | tf_op jit(solution)/shard_map/psum | solution.py:112
  420.0 90.2 %while.29 = (s32[]{:T(128)}, f32[9,2,1024,128]{3,2,1,0:T(8,128)}, s32[9,2]{1,0:T(8,128)S(1)}, bf16[9,2,1024,128]{3,2,1,0:T(8,128)(2,1)}, bf16[2,1024,128]{2,1,0:...) while((s32[]{:T(128)}, f32[9,2,1024,128]{3,2,1,0:T(8,128)}, ...), condition=%wide.region_21.22_spmd.clone, body=%wide.region_20.21_spmd.clone.sunk | while | flops 1098911744 | bytes 4761259 | solution.py:138
  421.7 8.3 %fusion.91 = f32[9,2,1024,128]{3,2,1,0:T(8,128)} fusion(f32[9,2,1024,128]{3,2,1,0:T(8,128)} %get-tuple-element.541, s32[]{:T(128)} %get-tuple-element.540, f32[2,1024]{1,0:T(2,128)S(1)} %dynamic-slice_bitcast_fusion.3, f32[2,1024]{1,0:T(2,128)S(1)} %get-tuple-element.556, pred[1024,1024]{0,1:T(8,128)(4,1)S(1)} %fusion.89, ...), kind=kOutput, calls=%fused_computation.39.clone.1 | convolution fusion | flops 1096810496 | bytes 3692032 | tf_op jit(solution)/shard_map/while/body/eval_jaxpr/aij,aje->aie/dot_general | solution.py:130
  431.7 8.3 %fusion.91 = f32[9,2,1024,128]{3,2,1,0:T(8,128)} fusion(f32[9,2,1024,128]{3,2,1,0:T(8,128)} %get-tuple-element.541, s32[]{:T(128)} %get-tuple-element.540, f32[2,1024]{1,0:T(2,128)S(1)} %dynamic-slice_bitcast_fusion.3, f32[2,1024]{1,0:T(2,128)S(1)} %get-tuple-element.556, pred[1024,1024]{0,1:T(8,128)(4,1)S(1)} %fusion.89, ...), kind=kOutput, calls=%fused_computation.39.clone.1 | convolution fusion | flops 1096810496 | bytes 3692032 | tf_op jit(solution)/shard_map/while/body/eval_jaxpr/aij,aje->aie/dot_general | solution.py:130
  441.7 8.3 %fusion.91 = f32[9,2,1024,128]{3,2,1,0:T(8,128)} fusion(f32[9,2,1024,128]{3,2,1,0:T(8,128)} %get-tuple-element.541, s32[]{:T(128)} %get-tuple-element.540, f32[2,1024]{1,0:T(2,128)S(1)} %dynamic-slice_bitcast_fusion.3, f32[2,1024]{1,0:T(2,128)S(1)} %get-tuple-element.556, pred[1024,1024]{0,1:T(8,128)(4,1)S(1)} %fusion.89, ...), kind=kOutput, calls=%fused_computation.39.clone.1 | convolution fusion | flops 1096810496 | bytes 3692032 | tf_op jit(solution)/shard_map/while/body/eval_jaxpr/aij,aje->aie/dot_general | solution.py:130
  451.7 8.3 %fusion.91 = f32[9,2,1024,128]{3,2,1,0:T(8,128)} fusion(f32[9,2,1024,128]{3,2,1,0:T(8,128)} %get-tuple-element.541, s32[]{:T(128)} %get-tuple-element.540, f32[2,1024]{1,0:T(2,128)S(1)} %dynamic-slice_bitcast_fusion.3, f32[2,1024]{1,0:T(2,128)S(1)} %get-tuple-element.556, pred[1024,1024]{0,1:T(8,128)(4,1)S(1)} %fusion.89, ...), kind=kOutput, calls=%fused_computation.39.clone.1 | convolution fusion | flops 1096810496 | bytes 3692032 | tf_op jit(solution)/shard_map/while/body/eval_jaxpr/aij,aje->aie/dot_general | solution.py:130
  461.7 8.3 %fusion.91 = f32[9,2,1024,128]{3,2,1,0:T(8,128)} fusion(f32[9,2,1024,128]{3,2,1,0:T(8,128)} %get-tuple-element.541, s32[]{:T(128)} %get-tuple-element.540, f32[2,1024]{1,0:T(2,128)S(1)} %dynamic-slice_bitcast_fusion.3, f32[2,1024]{1,0:T(2,128)S(1)} %get-tuple-element.556, pred[1024,1024]{0,1:T(8,128)(4,1)S(1)} %fusion.89, ...), kind=kOutput, calls=%fused_computation.39.clone.1 | convolution fusion | flops 1096810496 | bytes 3692032 | tf_op jit(solution)/shard_map/while/body/eval_jaxpr/aij,aje->aie/dot_general | solution.py:130
  471.7 8.3 %fusion.91 = f32[9,2,1024,128]{3,2,1,0:T(8,128)} fusion(f32[9,2,1024,128]{3,2,1,0:T(8,128)} %get-tuple-element.541, s32[]{:T(128)} %get-tuple-element.540, f32[2,1024]{1,0:T(2,128)S(1)} %dynamic-slice_bitcast_fusion.3, f32[2,1024]{1,0:T(2,128)S(1)} %get-tuple-element.556, pred[1024,1024]{0,1:T(8,128)(4,1)S(1)} %fusion.89, ...), kind=kOutput, calls=%fused_computation.39.clone.1 | convolution fusion | flops 1096810496 | bytes 3692032 | tf_op jit(solution)/shard_map/while/body/eval_jaxpr/aij,aje->aie/dot_general | solution.py:130
  481.7 8.3 %fusion.91 = f32[9,2,1024,128]{3,2,1,0:T(8,128)} fusion(f32[9,2,1024,128]{3,2,1,0:T(8,128)} %get-tuple-element.541, s32[]{:T(128)} %get-tuple-element.540, f32[2,1024]{1,0:T(2,128)S(1)} %dynamic-slice_bitcast_fusion.3, f32[2,1024]{1,0:T(2,128)S(1)} %get-tuple-element.556, pred[1024,1024]{0,1:T(8,128)(4,1)S(1)} %fusion.89, ...), kind=kOutput, calls=%fused_computation.39.clone.1 | convolution fusion | flops 1096810496 | bytes 3692032 | tf_op jit(solution)/shard_map/while/body/eval_jaxpr/aij,aje->aie/dot_general | solution.py:130
  491.8 8.4 %fusion.91 = f32[9,2,1024,128]{3,2,1,0:T(8,128)} fusion(f32[9,2,1024,128]{3,2,1,0:T(8,128)} %get-tuple-element.541, s32[]{:T(128)} %get-tuple-element.540, f32[2,1024]{1,0:T(2,128)S(1)} %dynamic-slice_bitcast_fusion.3, f32[2,1024]{1,0:T(2,128)S(1)} %get-tuple-element.556, pred[1024,1024]{0,1:T(8,128)(4,1)S(1)} %fusion.89, ...), kind=kOutput, calls=%fused_computation.39.clone.1 | convolution fusion | flops 1096810496 | bytes 3692032 | tf_op jit(solution)/shard_map/while/body/eval_jaxpr/aij,aje->aie/dot_general | solution.py:130
  501.8 8.4 %fusion.91 = f32[9,2,1024,128]{3,2,1,0:T(8,128)} fusion(f32[9,2,1024,128]{3,2,1,0:T(8,128)} %get-tuple-element.541, s32[]{:T(128)} %get-tuple-element.540, f32[2,1024]{1,0:T(2,128)S(1)} %dynamic-slice_bitcast_fusion.3, f32[2,1024]{1,0:T(2,128)S(1)} %get-tuple-element.556, pred[1024,1024]{0,1:T(8,128)(4,1)S(1)} %fusion.89, ...), kind=kOutput, calls=%fused_computation.39.clone.1 | convolution fusion | flops 1096810496 | bytes 3692032 | tf_op jit(solution)/shard_map/while/body/eval_jaxpr/aij,aje->aie/dot_general | solution.py:130
  510.2 4.3 reduce_sum.113
  514.5 0.9 multiply_convert_fusion
  (154 shorter events, 16.8 us)
Async XLA Ops:
  7.6 9.9 %copy-start.3 = (s32[256,8]{0,1:T(8,128)S(1)}, s32[256,8]{0,1:T(8,128)}, u32[]{:S(2)}) copy-start(s32[256,8]{0,1:T(8,128)} %param.12) | copy-start | bytes 24580
  7.7 10.1 %copy-start.4 = (s32[256,8]{0,1:T(8,128)S(1)}, s32[256,8]{0,1:T(8,128)}, u32[]{:S(2)}) copy-start(s32[256,8]{0,1:T(8,128)} %param.11) | copy-start | bytes 24580
  7.7 10.9 %copy-start = (s32[256]{0:T(256)S(1)}, s32[256]{0:T(256)}, u32[]{:S(2)}) copy-start(s32[256]{0:T(256)} %param.13) | copy-start | bytes 3076
  7.7 12.2 %copy-start.1 = (bf16[2,1024,128]{2,1,0:T(8,128)(2,1)S(1)}, bf16[2,1024,128]{2,1,0:T(8,128)(2,1)}, u32[]{:S(2)}) copy-start(bf16[2,1024,128]{2,1,0:T(8,128)(2,1)} %param.10) | copy-start | bytes 1572868
  7.7 12.2 %copy-start.2 = (bf16[2,1024,128]{2,1,0:T(8,128)(2,1)S(1)}, bf16[2,1024,128]{2,1,0:T(8,128)(2,1)}, u32[]{:S(2)}) copy-start(bf16[2,1024,128]{2,1,0:T(8,128)(2,1)} %param.9) | copy-start | bytes 1572868
  7.7 211.9 %all-to-all-start = ((bf16[32,2,1024,128]{3,2,1,0:T(8,128)(2,1)}), bf16[32,2,1024,128]{3,2,1,0:T(8,128)(2,1)}, u32[]{:S(2)}, u32[]{:S(2)}) async-start(bf16[32,2,1024,128]{3,2,1,0:T(8,128)(2,1)} %stack.2), calls=%async_computation | async-start | bytes 33554432 | tf_op jit(solution)/shard_map/all_to_all | solution.py:15
  309.8 22.7 %all-to-all-start.1 = ((f32[32,1,1024]{2,1,0:T(1,128)}), f32[32,1,1024]{2,1,0:T(1,128)S(1)}, u32[]{:S(2)}, u32[]{:S(2)}) async-start(f32[32,1,1024]{2,1,0:T(1,128)} %all_to_all.22), calls=%async_computation.1 | async-start | bytes 262144 | tf_op jit(solution)/shard_map/all_to_all | solution.py:87
  332.6 11.6 %all-to-all-start.2 = ((f32[32,1,1024]{2,1,0:T(1,128)}), f32[32,1,1024]{2,1,0:T(1,128)S(1)}, u32[]{:S(2)}, u32[]{:S(2)}) async-start(f32[32,1,1024]{2,1,0:T(1,128)} %all_to_all.24), calls=%async_computation.2 | async-start | bytes 262144 | tf_op jit(solution)/shard_map/all_to_all | solution.py:88
  347.9 71.4 %all-to-all-start.3 = ((f32[32,1,1024]{2,1,0:T(1,128)}), f32[32,1,1024]{2,1,0:T(1,128)S(1)}, u32[]{:S(2)}, u32[]{:S(2)}) async-start(f32[32,1,1024]{2,1,0:T(1,128)} %copy.101), calls=%async_computation.3 | async-start | bytes 262144 | tf_op jit(solution)/shard_map/all_to_all | solution.py:104
